TPU v7x, 512 devices: a whole 4x4x16 slice. The times are simulated.
512 devices in a mesh: loop: 32 (over z, y_hi), seg: 16 (over x, y_lo, core).
Axes of the slice: x: 4, y: 4 (y_hi: 2, y_lo: 2; y = y_hi * 2 + y_lo), z: 16, core: 2. Of those that a mesh axis runs over, the one named last changes fastest.
Arguments:
- dosage: bfloat16 [8192, 32768], P('seg', 'loop'), may hold values from -3 to 3
- weight_tiles: bfloat16 [3, 1024, 4096], P(None, None, 'loop'), may hold values from -0.109375 to 0.109375
- first_tile: int32 [4096], P('loop'), may hold values from 0 to 1
- last_tile: int32 [4096], P('loop'), may hold values from 1 to 2
Outputs:
- covariance: float32 [4096, 4096], P('seg', 'loop')
Inputs may be any that keep to these rules, and one draw needn't show every extreme that they name: `first_tile`: a gene's window always covers its home slot 1.
All inputs are finite; a program needn't handle non-finite values.
Results may differ from a plain program's by a relative error of at most 0.0021.
Values may be sent and summed in bfloat16 or wider, within the bound.
A program may use at most 64 MiB of HBM per device.

v0:
```python
import jax
import jax.numpy as jnp
from jax import lax
from jax.sharding import PartitionSpec as P


def shifted(value, axis, steps):
    count = lax.axis_size(axis)
    leading, last = (max(0, -steps), min(count, count - steps))
    return lax.ppermute(value, axis, [(source, source + steps) for source in range(leading, last)])


def shards(dosage, weight_tiles, first_tile, last_tile):
    n_slots = weight_tiles.shape[0]
    side_reach = (n_slots - 1) // 2
    slot_index = jnp.arange(n_slots, dtype=jnp.int32)[:, None]
    covered = (slot_index >= first_tile[None, :]) & (slot_index <= last_tile[None, :])
    masked = jnp.where(covered[:, None, :], weight_tiles, jnp.zeros((), weight_tiles.dtype))
    running = jnp.dot(dosage, masked[side_reach], preferred_element_type=jnp.float32)
    for slot_pos in range(n_slots):
        offset = slot_pos - side_reach
        if offset != 0:
            arrived = shifted(dosage, "loop", -offset)
            running = running + jnp.dot(
                arrived, masked[slot_pos], preferred_element_type=jnp.float32
            )
    projection = running.astype(jnp.bfloat16)
    pair_sums = lax.dot_general(
        lax.all_gather(projection, "loop", axis=1, tiled=True),
        projection,
        (((0,), (0,)), ((), ())),
        preferred_element_type=jnp.float32,
    )
    summed = lax.psum_scatter(pair_sums, "seg", scatter_dimension=0, tiled=True)
    sample_total = dosage.shape[0] * lax.axis_size("seg")
    return summed / sample_total


def solution(mesh):
    return jax.shard_map(
        shards,
        mesh=mesh,
        in_specs=(P("seg", "loop"), P(None, None, "loop"), P("loop"), P("loop")),
        out_specs=P("seg", "loop"),
        check_vma=False,
    )
```

profile of v0, /device:TPU:16, one launch (start us, length us, event | category | flops | bytes accessed | tf_op | source)
XLA Modules:
  0.0 306.9 jit_solution(11395456426967035104)
XLA Ops:
  6.5 0.0 all-gather.2.cloned.1.call-start
  6.5 3.6 %collective-permute-start = (bf16[512,1024]{1,0:T(8,128)(2,1)}, bf16[512,1024]{1,0:T(8,128)(2,1)S(1)}, u32[]{:S(2)}, u32[]{:S(2)}) collective-permute-start(bf16[512,1024]{1,0:T(8,128)(2,1)} %param.4), channel_id=1, source_target_pairs={{0,16},{16,32},{32,48},{48,64},{64,80},{80,96},{96,112},{112,128},... | collective-permute-start | bytes 3145736 | tf_op jit(solution)/shard_map/ppermute | solution.py:10
  10.1 5.4 %collective-permute-start.1 = (bf16[512,1024]{1,0:T(8,128)(2,1)}, bf16[512,1024]{1,0:T(8,128)(2,1)S(1)}, u32[]{:S(2)}, u32[]{:S(2)}) collective-permute-start(bf16[512,1024]{1,0:T(8,128)(2,1)} %param.4), channel_id=1, source_target_pairs={{16,0},{32,16},{48,32},{64,48},{80,64},{96,80},{112,96},{128,112},... | collective-permute-start | bytes 3145736 | tf_op jit(solution)/shard_map/ppermute | solution.py:10
  15.5 0.7 fusion.2
  16.2 1.2 broadcast_select_fusion
  17.4 1.7 fusion.1
  19.1 38.4 %collective-permute-done = bf16[512,1024]{1,0:T(8,128)(2,1)S(1)} collective-permute-done((bf16[512,1024]{1,0:T(8,128)(2,1)}, bf16[512,1024]{1,0:T(8,128)(2,1)S(1)}, u32[]{:S(2)}, u32[]{:S(2)}) %collective-permute-start) | collective-permute-done | bytes 1048608 | tf_op jit(solution)/shard_map/ppermute | solution.py:10
  57.5 0.5 convolution_add_fusion.1
  58.0 0.0 collective-permute-done.1
  58.0 1.1 fusion
  59.2 0.0 all-gather.2.cloned.1.call-update
  59.2 0.0 reduce-scatter.2.cloned.1.call-start
  59.2 165.9 %all-gather.2.cloned.1.call-done = bf16[512,4096]{0,1:T(8,128)(2,1)} async-done(((bf16[512,128]{0,1:T(8,128)(2,1)}), bf16[512,4096]{0,1:T(8,128)(2,1)}) %all-gather.2.cloned.1.call-update) | async-done | bytes 4194320 | tf_op jit(solution)/shard_map/all_gather | solution.py:29
  225.1 4.8 %fusion.3 = f32[4096,128]{1,0:T(8,128)} fusion(bf16[512,4096]{0,1:T(8,128)(2,1)} %all-gather.2.cloned.1.call-done, bf16[128,512]{1,0:T(8,128)(2,1)} %fusion), kind=kOutput, calls=%fused_computation.12 | convolution fusion | flops 536870912 | bytes 6422528 | tf_op jit(solution)/shard_map/dot_general | solution.py:28
  229.9 0.0 reduce-scatter.2.cloned.1.call-update
  229.9 68.5 %reduce-scatter.2.cloned.1.call-done = f32[256,128]{1,0:T(8,128)} async-done(((f32[4096,128]{1,0:T(8,128)}), f32[256,128]{1,0:T(8,128)}) %reduce-scatter.2.cloned.1.call-update) | async-done | bytes 131088 | tf_op jit(solution)/shard_map/reduce_scatter | solution.py:34
  298.4 1.6 broadcast_multiply_fusion
Async XLA Ops:
  6.5 218.6 %all-gather.2.cloned.1.call-start = ((), (), s32[]{:S(2)}) async-start(), calls=%async_computation.1 | async-start | bytes 4325376 | tf_op jit(solution)/shard_map/all_gather | solution.py:29
  6.5 51.0 %collective-permute-start = (bf16[512,1024]{1,0:T(8,128)(2,1)}, bf16[512,1024]{1,0:T(8,128)(2,1)S(1)}, u32[]{:S(2)}, u32[]{:S(2)}) collective-permute-start(bf16[512,1024]{1,0:T(8,128)(2,1)} %param.4), channel_id=1, source_target_pairs={{0,16},{16,32},{32,48},{48,64},{64,80},{80,96},{96,112},{112,128},... | collective-permute-start | bytes 3145736 | tf_op jit(solution)/shard_map/ppermute | solution.py:10
  10.1 47.9 %collective-permute-start.1 = (bf16[512,1024]{1,0:T(8,128)(2,1)}, bf16[512,1024]{1,0:T(8,128)(2,1)S(1)}, u32[]{:S(2)}, u32[]{:S(2)}) collective-permute-start(bf16[512,1024]{1,0:T(8,128)(2,1)} %param.4), channel_id=1, source_target_pairs={{16,0},{32,16},{48,32},{64,48},{80,64},{96,80},{112,96},{128,112},... | collective-permute-start | bytes 3145736 | tf_op jit(solution)/shard_map/ppermute | solution.py:10
  59.2 239.3 %reduce-scatter.2.cloned.1.call-start = ((), (), s32[]{:S(2)}) async-start(), calls=%async_computation.2 | async-start | bytes 2228224 | tf_op jit(solution)/shard_map/reduce_scatter | solution.py:34
Sparse Core Ops, SparseCore 0:
  59.3 165.7 all-gather.1
  230.0 68.3 reduce-scatter.1
where the time goes:
time: 307 us
  waiting for transfers between devices  273 us (89%)
  between operations  13.4 us (4%)
  starting transfers between devices  9.01 us (3%)
  matrix products  8.09 us (3%)
  other arithmetic  3.44 us (1%)
    all_gather x1, waiting for transfers between devices, shards(): lax.all_gather(projection, 'loop', axis=1, tiled=True)  166 us
    reduce_scatter x1, waiting for transfers between devices, shards(): summed = lax.psum_scatter(pair_sums, 'seg', scatter_dimension=0, tiled=True)  68.5 us
    ppermute x2, waiting for transfers between devices, shifted(): lax.ppermute(value, axis, [(source, source + steps) for source in range(l...  38.4 us
    ppermute x2, starting transfers between devices, shifted(): lax.ppermute(value, axis, [(source, source + steps) for source in range(l...  8.97 us
  transfers between devices with their start and end apart: 4, of which 3 were waited for; matrix products, arithmetic and copies ran while one was open for 1% of the time, Pallas kernels for 0%

commit v1 on v0

v1 whole, which is shorter than its diff:
```python
import functools

import jax
import jax.numpy as jnp
from jax import lax
from jax.experimental import pallas as pl
from jax.experimental.pallas import tpu as pltpu
from jax.sharding import PartitionSpec as P

MESH = pl.DeviceIdType.MESH
F32 = jnp.float32
BF16 = jnp.bfloat16
XS, ZS = 4, 16


def device(x, t, lo, z, c):
    return {"loop": 2 * z + t, "seg": 4 * x + 2 * lo + c}


def kernel(
    dosage, tiles, first, last, out,
    mine, send_a, send_b, tile_a, tile_b,
    part_y, part_z, got_y, got_z, held,
    columns, rows, shares, across, summed, arrived, landed,
    wsend, wrecv, csend, crecv, psend, precv,
    qsend, qrecv, rsend, rrecv, osend, orecv,
    xsend, xrecv, ysend, yrecv,
):
    loop, seg = lax.axis_index("loop"), lax.axis_index("seg")
    z, t = loop // 2, loop % 2
    x, lo, c = seg // 4, (seg // 2) % 2, seg % 2
    sign = 1 - 2 * t
    z_fore, z_back = (z + sign + ZS) % ZS, (z - sign + ZS) % ZS
    fore, back = device(x, t, lo, z_fore, c), device(x, t, lo, z_back, c)
    twin = device(x, t, lo, z, 1 - c)
    pair = device(x, 1 - t, lo, z, c)
    near = device(x, 1 - t, 1 - lo, z, c)
    near_back = device(x, 1 - t, 1 - lo, z_back, c)
    side = device(x, t, 1 - lo, z, c)
    half = dosage.shape[0] // 2
    depth = dosage.shape[1]
    gene = tiles.shape[2]

    barrier = pltpu.get_barrier_semaphore()
    partners = [fore, back, twin, pair, near, near_back, side]
    partners += [device((x + k) % XS, t, lo, z, c) for k in range(1, XS)]
    for partner in partners:
        pl.semaphore_signal(barrier, inc=1, device_id=partner, device_id_type=MESH)

    def remote(src, dst, send, recv, to):
        return pltpu.make_async_remote_copy(
            src_ref=src, dst_ref=dst, send_sem=send, recv_sem=recv,
            device_id=to, device_id_type=MESH,
        )

    low, high = first[...], last[...]

    def mask(slot):
        block = loop + slot - 1
        ok = (low <= slot) & (high >= slot) & (block >= 0) & (block < 2 * ZS)
        return jnp.where(ok, 1.0, 0.0).astype(BF16)

    piece = pl.ds(pl.multiple_of(c * (depth // 2), depth // 2), depth // 2)
    slot_b, slot_a = 2 * t, 2 - 2 * t
    send_b[...] = tiles[slot_b, piece, :] * mask(slot_b)
    send_a[...] = tiles[slot_a, piece, :] * mask(slot_a)
    pl.semaphore_wait(barrier, len(partners))

    weights = []
    for i, (src, dst, to) in enumerate(
        ((send_b, tile_b, near_back), (send_a, tile_a, near))
    ):
        copy = remote(src, dst.at[piece], wsend.at[i], wrecv.at[i], to)
        copy.start()
        weights.append(copy)
    mine[...] = tiles[1] * mask(1)
    partials = []
    for k in range(2):
        span = pl.ds(k * half, half)
        part_y[span, :] = jnp.dot(dosage[span, :], mine[...], preferred_element_type=F32)
        copy = remote(part_y.at[span], got_y.at[span], psend.at[k], precv.at[k], pair)
        copy.start()
        partials.append(copy)

    swaps = []
    for i, dst in enumerate((tile_b, tile_a)):
        weights[i].wait_recv()
        copy = remote(dst.at[piece], dst.at[piece], csend.at[i], crecv.at[i], twin)
        copy.start()
        swaps.append(copy)
        copy.wait_recv()
        for k in range(2):
            span = pl.ds(k * half, half)
            value = jnp.dot(dosage[span, :], dst[...], preferred_element_type=F32)
            if i == 0:
                part_z[span, :] = value
                copy = remote(part_z.at[span], got_z.at[span], psend.at[2 + k], precv.at[2 + k], back)
                copy.start()
                partials.append(copy)
            else:
                held[span, :] = value

    lead = (z + c) % 2 == 0
    cols_own = pl.ds(pl.multiple_of((1 - t) * gene, gene), gene)
    cols_other = pl.ds(pl.multiple_of(t * gene, gene), gene)
    place = z // 2

    def ring(block, flow, step, j, to):
        chunk = rows.at[block, j]
        return remote(
            chunk, chunk, rsend.at[flow, step // 2, j], rrecv.at[flow, (step + 1) // 2, j], to
        )

    def start_ring(j):
        ring(place, 0, 0, j, fore).start()
        ring(place, 1, 0, j, back).start()

    locals_ = []
    for k in range(2):
        span = pl.ds(k * half, half)
        partials[k].wait_recv()
        partials[2 + k].wait_recv()
        value = held[span, :] + got_y[span, :] + got_z[span, :]
        columns[span, cols_own] = value.astype(BF16)
        turned = value.T.astype(BF16)

        @pl.when(lead)
        def _():
            rows[place, k] = turned
            start_ring(k)

        @pl.when(jnp.logical_not(lead))
        def _():
            landed[k] = turned
            remote(landed.at[k], rows.at[place, 2 + k], osend.at[k], orecv.at[k], twin).start()

        here = columns.at[span, cols_own]
        copy = remote(here, here, qsend.at[0, k], qrecv.at[0, k], pair)
        copy.start()
        locals_.append(copy)
        there = columns.at[pl.ds(2 * half + k * half, half), cols_own]
        copy = remote(here, there, qsend.at[1, k], qrecv.at[1, k], twin)
        copy.start()
        locals_.append(copy)

    @pl.when(lead)
    def _():
        for k in range(2):
            remote(landed.at[k], rows.at[place, 2 + k], osend.at[k], orecv.at[k], twin).wait_recv()
            start_ring(2 + k)

    relays = []
    for k in range(2):
        span = pl.ds(k * half, half)
        got = columns.at[span, cols_other]
        remote(got, got, qsend.at[0, k], qrecv.at[0, k], pair).wait_recv()
        there = columns.at[pl.ds(2 * half + k * half, half), cols_other]
        copy = remote(got, there, qsend.at[2, k], qrecv.at[2, k], twin)
        copy.start()
        relays.append(copy)
    for copy in (locals_[1], locals_[3], *relays):
        copy.wait_recv()

    def share(block):
        turned = jnp.concatenate([rows[block, j] for j in range(4)], axis=1)
        shares[block] = jnp.dot(turned, columns[...], preferred_element_type=F32)
        home = block // 2

        @pl.when(home != x)
        def _():
            remote(
                shares.at[block], across.at[block % 2, x], xsend.at[block],
                xrecv.at[block % 2, x], device(home, t, lo, z, c),
            ).start()

    @pl.when(lead)
    def _():
        share(place)

    odd = (z + c) % 2

    def travel(i, carry):
        step = 2 * i + odd
        far = (z - sign * step + 2 * ZS) % ZS // 2
        close = (z + sign * step + 2 * ZS) % ZS // 2
        for j in range(4):
            @pl.when((step >= 1) & (step <= 8))
            def _():
                ring(far, 0, step - 1, j, fore).wait_recv()

            @pl.when((step >= 1) & (step <= 7))
            def _():
                ring(far, 0, step, j, fore).start()
                ring(close, 1, step - 1, j, back).wait_recv()

            @pl.when((step >= 1) & (step <= 6))
            def _():
                ring(close, 1, step, j, back).start()

        @pl.when((step >= 1) & (step <= 8))
        def _():
            share(far)

        @pl.when((step >= 1) & (step <= 7))
        def _():
            share(close)

        return carry

    lax.fori_loop(0, 5, travel, 0)

    for other in range(2):
        block = 2 * x + other
        total = shares[block]
        for k in range(1, XS):
            source = (x + k) % XS
            remote(
                shares.at[block], across.at[other, source], xsend.at[block],
                xrecv.at[other, source], twin,
            ).wait_recv()
            total = total + across[other, source]
        for way in range(2):
            summed[other, way] = total[:, way * gene:(way + 1) * gene]
    outs = []
    for flip_t, flip_lo, index in ((1, 0, 0), (0, 1, 1), (1, 1, 2)):
        to_t, to_lo = (t + flip_t) % 2, (lo + flip_lo) % 2
        copy = remote(
            summed.at[to_lo, to_t], arrived.at[index], ysend.at[index], yrecv.at[index],
            device(x, to_t, to_lo, z, c),
        )
        copy.start()
        outs.append(copy)
    scale = 1.0 / (2 * half * XS * 4)
    own_rows = pl.ds(pl.multiple_of((1 - t) * gene, gene), gene)
    other_rows = pl.ds(pl.multiple_of(t * gene, gene), gene)
    outs[1].wait_recv()
    out[own_rows, :] = (summed[lo, t] + arrived[1]) * scale
    outs[0].wait_recv()
    outs[2].wait_recv()
    out[other_rows, :] = (arrived[0] + arrived[2]) * scale

    for copy in (*weights, *swaps, *partials, *locals_, *relays, *outs):
        copy.wait_send()

    @pl.when(jnp.logical_not(lead))
    def _():
        for k in range(2):
            remote(landed.at[k], rows.at[place, 2 + k], osend.at[k], orecv.at[k], twin).wait_send()

    @pl.when(lead)
    def _():
        for j in range(4):
            ring(place, 0, 0, j, fore).wait_send()
            ring(place, 1, 0, j, back).wait_send()

    def drain(i, carry):
        step = 2 * i + odd
        for j in range(4):
            @pl.when((step >= 1) & (step <= 7))
            def _():
                ring(place, 0, step, j, fore).wait_send()

            @pl.when((step >= 1) & (step <= 6))
            def _():
                ring(place, 1, step, j, back).wait_send()

        return carry

    lax.fori_loop(0, 4, drain, 0)

    def drain_shares(block, carry):
        @pl.when(block // 2 != x)
        def _():
            remote(
                shares.at[block], across.at[0, 0], xsend.at[block], xrecv.at[0, 0], twin
            ).wait_send()

        return carry

    lax.fori_loop(0, ZS // 2, drain_shares, 0)


def shards(dosage, weight_tiles, first_tile, last_tile):
    samples, depth = dosage.shape
    gene = weight_tiles.shape[2]
    half = samples // 2
    dma = pltpu.SemaphoreType.DMA
    vmem = pl.BlockSpec(memory_space=pltpu.VMEM)
    return pl.pallas_call(
        kernel,
        out_shape=jax.ShapeDtypeStruct((2 * gene, gene), F32),
        in_specs=[vmem] * 4,
        out_specs=vmem,
        scratch_shapes=[
            pltpu.VMEM((depth, gene), BF16),
            pltpu.VMEM((depth // 2, gene), BF16),
            pltpu.VMEM((depth // 2, gene), BF16),
            pltpu.VMEM((depth, gene), BF16),
            pltpu.VMEM((depth, gene), BF16),
            pltpu.VMEM((samples, gene), F32),
            pltpu.VMEM((samples, gene), F32),
            pltpu.VMEM((samples, gene), F32),
            pltpu.VMEM((samples, gene), F32),
            pltpu.VMEM((samples, gene), F32),
            pltpu.VMEM((2 * samples, 2 * gene), BF16),
            pltpu.VMEM((ZS // 2, 4, gene, half), BF16),
            pltpu.VMEM((ZS // 2, gene, 2 * gene), F32),
            pltpu.VMEM((2, XS, gene, 2 * gene), F32),
            pltpu.VMEM((2, 2, gene, gene), F32),
            pltpu.VMEM((3, gene, gene), F32),
            pltpu.VMEM((2, gene, half), BF16),
            dma((2,)), dma((2,)), dma((2,)), dma((2,)),
            dma((4,)), dma((4,)),
            dma((3, 2)), dma((3, 2)),
            dma((2, 5, 4)), dma((2, 5, 4)),
            dma((2,)), dma((2,)),
            dma((ZS // 2,)), dma((2, XS)),
            dma((3,)), dma((3,)),
        ],
        compiler_params=pltpu.CompilerParams(
            collective_id=0, has_side_effects=True, vmem_limit_bytes=40 * 2**20
        ),
    )(dosage, weight_tiles, first_tile.reshape(1, gene), last_tile.reshape(1, gene))


def solution(mesh):
    return jax.shard_map(
        shards,
        mesh=mesh,
        in_specs=(P("seg", "loop"), P(None, None, "loop"), P("loop"), P("loop")),
        out_specs=P("seg", "loop"),
        check_vma=False,
    )
```

time: 307 us -> 77.9 us (0.25)
  the two profiles are of different devices: /device:TPU:16 before, /device:TPU:4 now
where the time goes in v1:
time: 77.9 us; the launch traced here: 77.7 us
  Pallas kernels  74 us (95%)
  local copies, waits for them, and re-layouts  3.68 us (5%)
    pallas_call x1, Pallas kernels, shards(): pl.pallas_call(kernel, out_shape=jax.ShapeDtypeStruct((2 * gene, gene), F...  74 us
    unnamed x9, local copies, waits for them, and re-layouts  3.68 us

profile of v1, /device:TPU:4, one launch (start us, length us, event | category | flops | bytes accessed | tf_op | source)
XLA Modules:
  0.0 77.7 jit_solution(797166480564894583)
XLA Ops:
  0.0 0.0 copy-start.2
  0.0 0.0 copy-start.3
  0.0 0.7 copy-done.2
  0.7 0.0 copy-done.3
  0.7 0.0 copy-start
  0.7 1.2 %copy-done = bf16[512,1024]{1,0:T(8,128)(2,1)S(1)} copy-done((bf16[512,1024]{1,0:T(8,128)(2,1)S(1)}, bf16[512,1024]{1,0:T(8,128)(2,1)}, u32[]{:S(2)}) %copy-start) | copy-done | bytes 1048600
  1.9 0.0 copy-start.1
  1.9 1.1 %copy-done.1 = bf16[3,1024,128]{2,1,0:T(8,128)(2,1)S(1)} copy-done((bf16[3,1024,128]{2,1,0:T(8,128)(2,1)S(1)}, bf16[3,1024,128]{2,1,0:T(8,128)(2,1)}, u32[]{:S(2)}) %copy-start.1) | copy-done | bytes 786456
  3.0 74.0 %shard_map.46 = f32[256,128]{1,0:T(8,128)S(1)} custom-call(bf16[512,1024]{1,0:T(8,128)(2,1)S(1)} %copy-done, bf16[3,1024,128]{2,1,0:T(8,128)(2,1)S(1)} %copy-done.1, s32[1,128]{1,0:T(1,128)S(1)} %bitcast.2, s32[1,128]{1,0:T(1,128)S(1)} %bitcast.3), custom_call_target="tpu_custom_call" | custom-call | tf_op jit(solution)/shard_map/pallas_call | solution.py:289
  77.0 0.7 copy.6
Async XLA Ops:
  0.0 0.7 copy-start.2
  0.0 0.7 copy-start.3
  0.7 1.2 %copy-start = (bf16[512,1024]{1,0:T(8,128)(2,1)S(1)}, bf16[512,1024]{1,0:T(8,128)(2,1)}, u32[]{:S(2)}) copy-start(bf16[512,1024]{1,0:T(8,128)(2,1)} %dosage.1) | copy-start | bytes 3145732
  1.9 1.1 %copy-start.1 = (bf16[3,1024,128]{2,1,0:T(8,128)(2,1)S(1)}, bf16[3,1024,128]{2,1,0:T(8,128)(2,1)}, u32[]{:S(2)}) copy-start(bf16[3,1024,128]{2,1,0:T(8,128)(2,1)} %tiles.1) | copy-start | bytes 2359300

commit v2 on v1

v2 whole, which is shorter than its diff:
```python
import functools

import jax
import jax.numpy as jnp
from jax import lax
from jax.experimental import pallas as pl
from jax.experimental.pallas import tpu as pltpu
from jax.sharding import PartitionSpec as P

MESH = pl.DeviceIdType.MESH
F32 = jnp.float32
BF16 = jnp.bfloat16
XS, ZS = 4, 16


def device(x, t, lo, z, c):
    return {"loop": 2 * z + t, "seg": 4 * x + 2 * lo + c}


ORDER = (0, 1, 4, 2, 5, 3, 6, 7)
PARTS = 4


def kernel(
    dosage_hbm, tiles_hbm, first_hbm, last_hbm, out,
    dosage, tiles, first, last,
    mine, send_a, send_b, tile_a, tile_b,
    part_y, part_z, got_y, got_z, held,
    columns, rows, shares, across, summed, arrived, landed,
    isem, wsend, wrecv, csend, crecv, psend, precv, zsend, zrecv,
    qsend, qrecv, rsend, rrecv, osend, orecv,
    xsend, xrecv, ysend, yrecv,
):
    loop, seg = lax.axis_index("loop"), lax.axis_index("seg")
    z, t = loop // 2, loop % 2
    x, lo, c = seg // 4, (seg // 2) % 2, seg % 2
    sign = 1 - 2 * t
    z_fore, z_back = (z + sign + ZS) % ZS, (z - sign + ZS) % ZS
    fore, back = device(x, t, lo, z_fore, c), device(x, t, lo, z_back, c)
    fore_twin, back_twin = device(x, t, lo, z_fore, 1 - c), device(x, t, lo, z_back, 1 - c)
    twin = device(x, t, lo, z, 1 - c)
    pair = device(x, 1 - t, lo, z, c)
    near = device(x, 1 - t, 1 - lo, z, c)
    near_back = device(x, 1 - t, 1 - lo, z_back, c)
    side = device(x, t, 1 - lo, z, c)
    samples, depth = dosage.shape
    gene = tiles.shape[2]
    part = samples // PARTS
    half = samples // 2

    barrier = pltpu.get_barrier_semaphore()
    partners = [fore, back, fore_twin, back_twin, twin, pair, near, near_back, side]
    partners += [device((x + k) % XS, t, lo, z, c) for k in range(1, XS)]
    for partner in partners:
        pl.semaphore_signal(barrier, inc=1, device_id=partner, device_id_type=MESH)

    piece = pl.ds(pl.multiple_of(c * (depth // 2), depth // 2), depth // 2)
    slot_b, slot_a = 2 * t, 2 - 2 * t
    loads = [
        pltpu.make_async_copy(src, dst, isem.at[i])
        for i, (src, dst) in enumerate((
            (first_hbm, first), (last_hbm, last),
            (tiles_hbm.at[slot_b, piece], tiles.at[slot_b, piece]),
            (tiles_hbm.at[slot_a, piece], tiles.at[slot_a, piece]),
            (tiles_hbm.at[1], tiles.at[1]), (dosage_hbm, dosage),
        ))
    ]
    for load in loads:
        load.start()

    def remote(src, dst, send, recv, to):
        return pltpu.make_async_remote_copy(
            src_ref=src, dst_ref=dst, send_sem=send, recv_sem=recv,
            device_id=to, device_id_type=MESH,
        )

    loads[0].wait()
    loads[1].wait()
    low, high = first[...], last[...]

    def mask(slot):
        block = loop + slot - 1
        ok = (low <= slot) & (high >= slot) & (block >= 0) & (block < 2 * ZS)
        return jnp.where(ok, 1.0, 0.0).astype(BF16)

    loads[2].wait()
    send_b[...] = tiles[slot_b, piece, :] * mask(slot_b)
    pl.semaphore_wait(barrier, len(partners))

    give_b = remote(send_b, tile_b.at[piece], wsend.at[0], wrecv.at[0], near_back)
    give_b.start()
    loads[3].wait()
    send_a[...] = tiles[slot_a, piece, :] * mask(slot_a)
    give_a = remote(send_a, tile_a.at[piece], wsend.at[1], wrecv.at[1], near)
    give_a.start()
    loads[4].wait()
    mine[...] = tiles[1] * mask(1)
    loads[5].wait()
    partials = []

    def send_partials():
        for k in range(2):
            span = pl.ds(k * half, half)
            copy = remote(part_y.at[span], got_y.at[span], psend.at[k], precv.at[k], pair)
            copy.start()
            partials.append(copy)

    part_y[...] = jnp.dot(dosage[...], mine[...], preferred_element_type=F32)
    swap_b = remote(tile_b.at[piece], tile_b.at[piece], csend.at[0], crecv.at[0], twin)
    swap_a = remote(tile_a.at[piece], tile_a.at[piece], csend.at[1], crecv.at[1], twin)
    give_b.wait_recv()
    swap_b.start()
    send_partials()
    swap_b.wait_recv()
    halos = []
    for k in range(PARTS):
        span = pl.ds(k * part, part)
        part_z[span, :] = jnp.dot(dosage[span, :], tile_b[...], preferred_element_type=F32)
        copy = remote(part_z.at[span], got_z.at[span], zsend.at[k], zrecv.at[k], back)
        copy.start()
        halos.append(copy)
    give_a.wait_recv()
    swap_a.start()
    swap_a.wait_recv()
    held[...] = jnp.dot(dosage[...], tile_a[...], preferred_element_type=F32)

    lead = (z + c) % 2 == 0
    cols_own = pl.ds(pl.multiple_of((1 - t) * gene, gene), gene)
    cols_other = pl.ds(pl.multiple_of(t * gene, gene), gene)
    place = z // 2

    def ring(block, flow, step, j, to):
        chunk = rows.at[block, j]
        return remote(
            chunk, chunk, rsend.at[flow, step // 2, j], rrecv.at[flow, (step + 1) // 2, j], to
        )

    def enter(k, flow, to):
        return remote(
            landed.at[k], rows.at[place, PARTS + k], osend.at[flow, k],
            rrecv.at[flow, 0, PARTS + k], to,
        )

    def enter_twin(k):
        return remote(
            landed.at[k], rows.at[place, PARTS + k], osend.at[2, k], orecv.at[k], twin
        )

    locals_ = []
    for k in range(PARTS):
        span = pl.ds(k * part, part)
        if k % 2 == 0:
            partials[k // 2].wait_recv()
        halos[k].wait_recv()
        value = held[span, :] + got_y[span, :] + got_z[span, :]
        turned = value.T.astype(BF16)

        @pl.when(lead)
        def _():
            rows[place, k] = turned
            ring(place, 0, 0, k, fore).start()
            ring(place, 1, 0, k, back).start()

        @pl.when(jnp.logical_not(lead))
        def _():
            landed[k] = turned
            enter(k, 0, fore_twin).start()
            enter(k, 1, back_twin).start()
            enter_twin(k).start()

        columns[span, cols_own] = value.astype(BF16)
        if k % 2 == 1:
            i = k // 2
            here = columns.at[pl.ds(i * half, half), cols_own]
            copy = remote(here, here, qsend.at[0, i], qrecv.at[0, i], pair)
            copy.start()
            locals_.append(copy)
            there = columns.at[pl.ds(samples + i * half, half), cols_own]
            copy = remote(here, there, qsend.at[1, i], qrecv.at[1, i], twin)
            copy.start()
            locals_.append(copy)

    def share(block):
        turned = jnp.concatenate([rows[block, j] for j in range(2 * PARTS)], axis=1)
        shares[block] = jnp.dot(turned, columns[...], preferred_element_type=F32)
        home = block // 2

        @pl.when(home != x)
        def _():
            remote(
                shares.at[block], across.at[block % 2, x], xsend.at[block],
                xrecv.at[block % 2, x], device(home, t, lo, z, c),
            ).start()

    odd = (z + c) % 2

    def pass_on(step, far, close):
        for j in ORDER:
            @pl.when((step >= 1) & (step <= 8))
            def _():
                ring(far, 0, step - 1, j, fore).wait_recv()

            @pl.when((step >= 1) & (step <= 7))
            def _():
                ring(far, 0, step, j, fore).start()
                ring(close, 1, step - 1, j, back).wait_recv()

            @pl.when((step >= 1) & (step <= 6))
            def _():
                ring(close, 1, step, j, back).start()

    def spots(step):
        return (z - sign * step + 2 * ZS) % ZS // 2, (z + sign * step + 2 * ZS) % ZS // 2

    pass_on(odd, *spots(odd))
    relays = []
    for i in range(2):
        got = columns.at[pl.ds(i * half, half), cols_other]
        remote(got, got, qsend.at[0, i], qrecv.at[0, i], pair).wait_recv()
        there = columns.at[pl.ds(samples + i * half, half), cols_other]
        copy = remote(got, there, qsend.at[2, i], qrecv.at[2, i], twin)
        copy.start()
        relays.append(copy)
    for copy in (locals_[1], locals_[3], *relays):
        copy.wait_recv()

    @pl.when(lead)
    def _():
        for k in range(PARTS):
            enter_twin(k).wait_recv()
        share(place)

    @pl.when(jnp.logical_not(lead))
    def _():
        for block in spots(1):
            share(block)

    def travel(i, carry):
        step = 2 * i + odd
        far, close = spots(step)
        pass_on(step, far, close)

        @pl.when(step <= 8)
        def _():
            share(far)

        @pl.when(step <= 7)
        def _():
            share(close)

        return carry

    lax.fori_loop(1, 5, travel, 0)

    def away(block):
        gap = (2 * block + c - z + ZS) % ZS
        return jnp.minimum(gap, ZS - gap)

    swapped = (away(2 * x) > away(2 * x + 1)).astype(jnp.int32)

    def ysend_copy(index, block_lo, to_t, to_lo):
        return remote(
            summed.at[block_lo, to_t], arrived.at[index], ysend.at[index], yrecv.at[index],
            device(x, to_t, to_lo, z, c),
        )

    same = ysend_copy(0, lo, 1 - t, lo)
    cross = ysend_copy(1, 1 - lo, t, 1 - lo)
    both = ysend_copy(2, 1 - lo, 1 - t, 1 - lo)
    for turn in range(2):
        other = (swapped + turn) % 2
        block = 2 * x + other
        for k in range(1, XS):
            source = (x + k) % XS
            remote(
                shares.at[block], across.at[other, source], xsend.at[block],
                xrecv.at[other, source], twin,
            ).wait_recv()
        total = shares[block]
        for k in range(1, XS):
            total = total + across[other, (x + k) % XS]
        for way in range(2):
            summed[other, way] = total[:, way * gene:(way + 1) * gene]

        @pl.when(other == lo)
        def _():
            same.start()

        @pl.when(other != lo)
        def _():
            both.start()
            cross.start()

    scale = 1.0 / (samples * XS * 4)
    own_rows = pl.ds(pl.multiple_of((1 - t) * gene, gene), gene)
    other_rows = pl.ds(pl.multiple_of(t * gene, gene), gene)
    cross.wait_recv()
    out[own_rows, :] = (summed[lo, t] + arrived[1]) * scale
    same.wait_recv()
    both.wait_recv()
    out[other_rows, :] = (arrived[0] + arrived[2]) * scale

    for copy in (
        give_a, give_b, swap_a, swap_b, *partials, *halos, *locals_, *relays, same, cross, both
    ):
        copy.wait_send()

    @pl.when(jnp.logical_not(lead))
    def _():
        for k in range(PARTS):
            enter(k, 0, fore_twin).wait_send()
            enter(k, 1, back_twin).wait_send()
            enter_twin(k).wait_send()

    @pl.when(lead)
    def _():
        for k in range(PARTS):
            ring(place, 0, 0, k, fore).wait_send()
            ring(place, 1, 0, k, back).wait_send()

    def drain(i, carry):
        step = 2 * i + odd
        for j in range(2 * PARTS):
            @pl.when((step >= 1) & (step <= 7))
            def _():
                ring(place, 0, step, j, fore).wait_send()

            @pl.when((step >= 1) & (step <= 6))
            def _():
                ring(place, 1, step, j, back).wait_send()

        return carry

    lax.fori_loop(0, 4, drain, 0)

    def drain_shares(block, carry):
        @pl.when(block // 2 != x)
        def _():
            remote(
                shares.at[block], across.at[0, 0], xsend.at[block], xrecv.at[0, 0], twin
            ).wait_send()

        return carry

    lax.fori_loop(0, ZS // 2, drain_shares, 0)


def shards(dosage, weight_tiles, first_tile, last_tile):
    samples, depth = dosage.shape
    gene = weight_tiles.shape[2]
    part = samples // PARTS
    dma = pltpu.SemaphoreType.DMA
    vmem = pl.BlockSpec(memory_space=pltpu.VMEM)
    return pl.pallas_call(
        kernel,
        out_shape=jax.ShapeDtypeStruct((2 * gene, gene), F32),
        in_specs=[pl.BlockSpec(memory_space=pltpu.HBM)] * 4,
        out_specs=vmem,
        scratch_shapes=[
            pltpu.VMEM((samples, depth), BF16),
            pltpu.VMEM((3, depth, gene), BF16),
            pltpu.VMEM((1, gene), jnp.int32),
            pltpu.VMEM((1, gene), jnp.int32),
            pltpu.VMEM((depth, gene), BF16),
            pltpu.VMEM((depth // 2, gene), BF16),
            pltpu.VMEM((depth // 2, gene), BF16),
            pltpu.VMEM((depth, gene), BF16),
            pltpu.VMEM((depth, gene), BF16),
            pltpu.VMEM((samples, gene), F32),
            pltpu.VMEM((samples, gene), F32),
            pltpu.VMEM((samples, gene), F32),
            pltpu.VMEM((samples, gene), F32),
            pltpu.VMEM((samples, gene), F32),
            pltpu.VMEM((2 * samples, 2 * gene), BF16),
            pltpu.VMEM((ZS // 2, 2 * PARTS, gene, part), BF16),
            pltpu.VMEM((ZS // 2, gene, 2 * gene), F32),
            pltpu.VMEM((2, XS, gene, 2 * gene), F32),
            pltpu.VMEM((2, 2, gene, gene), F32),
            pltpu.VMEM((3, gene, gene), F32),
            pltpu.VMEM((PARTS, gene, part), BF16),
            dma((6,)), dma((2,)), dma((2,)), dma((2,)), dma((2,)),
            dma((2,)), dma((2,)), dma((PARTS,)), dma((PARTS,)),
            dma((3, 2)), dma((3, 2)),
            dma((2, 4, 2 * PARTS)), dma((2, 5, 2 * PARTS)),
            dma((3, PARTS)), dma((PARTS,)),
            dma((ZS // 2,)), dma((2, XS)),
            dma((3,)), dma((3,)),
        ],
        compiler_params=pltpu.CompilerParams(
            collective_id=0, has_side_effects=True, vmem_limit_bytes=60 * 2**20
        ),
    )(dosage, weight_tiles, first_tile.reshape(1, gene), last_tile.reshape(1, gene))


def solution(mesh):
    return jax.shard_map(
        shards,
        mesh=mesh,
        in_specs=(P("seg", "loop"), P(None, None, "loop"), P("loop"), P("loop")),
        out_specs=P("seg", "loop"),
        check_vma=False,
    )
```

time: 77.9 us -> 72.2 us (0.927)
  the two profiles are of different devices: /device:TPU:4 before, /device:TPU:44 now
where the time goes in v2:
time: 72.2 us; the launch traced here: 72.1 us
  Pallas kernels  70.5 us (98%)
  local copies, waits for them, and re-layouts  1.57 us (2%)
    pallas_call x1, Pallas kernels, shards(): pl.pallas_call(kernel, out_shape=jax.ShapeDtypeStruct((2 * gene, gene), F...  70.5 us
    unnamed x1, local copies, waits for them, and re-layouts  1.57 us

profile of v2, /device:TPU:44, one launch (start us, length us, event | category | flops | bytes accessed | tf_op | source)
XLA Modules:
  0.0 72.1 jit_solution(13906216439548707407)
XLA Ops:
  0.0 70.5 %shard_map.46 = f32[256,128]{1,0:T(8,128)} custom-call(bf16[512,1024]{1,0:T(8,128)(2,1)} %dosage_hbm.1, bf16[3,1024,128]{2,1,0:T(8,128)(2,1)} %tiles_hbm.1, s32[1,128]{1,0:T(1,128)} %bitcast.2, s32[1,128]{1,0:T(1,128)} %bitcast.3), custom_call_target="tpu_custom_call" | custom-call | tf_op jit(solution)/shard_map/pallas_call | solution.py:354
  70.5 1.6 %copy.6 = f32[256,128]{1,0:T(8,128)} copy(f32[256,128]{1,0:T(8,128)} %shard_map.46) | data formatting | bytes 262144

commit v3 on v2

--- a/solution.py
+++ b/solution.py
@@ -19,6 +19,10 @@
 
 ORDER = (0, 1, 4, 2, 5, 3, 6, 7)
 PARTS = 4
+
+
+def reach(flow, j):
+    return 8 - flow
 
 
 def kernel(
@@ -182,32 +186,31 @@
 
     def share(block):
         turned = jnp.concatenate([rows[block, j] for j in range(2 * PARTS)], axis=1)
-        shares[block] = jnp.dot(turned, columns[...], preferred_element_type=F32)
+        value = jnp.dot(turned, columns[...], preferred_element_type=F32)
+        for way in range(2):
+            shares[block, way] = value[:, way * gene:(way + 1) * gene]
         home = block // 2
 
         @pl.when(home != x)
         def _():
-            remote(
-                shares.at[block], across.at[block % 2, x], xsend.at[block],
-                xrecv.at[block % 2, x], device(home, t, lo, z, c),
-            ).start()
+            for way in range(2):
+                remote(
+                    shares.at[block, way], across.at[block % 2, x, way], xsend.at[block, way],
+                    xrecv.at[block % 2, x, way], device(home, t, lo, z, c),
+                ).start()
 
     odd = (z + c) % 2
 
     def pass_on(step, far, close):
         for j in ORDER:
-            @pl.when((step >= 1) & (step <= 8))
-            def _():
-                ring(far, 0, step - 1, j, fore).wait_recv()
-
-            @pl.when((step >= 1) & (step <= 7))
-            def _():
-                ring(far, 0, step, j, fore).start()
-                ring(close, 1, step - 1, j, back).wait_recv()
-
-            @pl.when((step >= 1) & (step <= 6))
-            def _():
-                ring(close, 1, step, j, back).start()
+            for flow, block, to in ((0, far, fore), (1, close, back)):
+                @pl.when((step >= 1) & (step <= reach(flow, j)))
+                def _():
+                    ring(block, flow, step - 1, j, to).wait_recv()
+
+                @pl.when((step >= 1) & (step < reach(flow, j)))
+                def _():
+                    ring(block, flow, step, j, to).start()
 
     def spots(step):
         return (z - sign * step + 2 * ZS) % ZS // 2, (z + sign * step + 2 * ZS) % ZS // 2
@@ -270,26 +273,29 @@
     for turn in range(2):
         other = (swapped + turn) % 2
         block = 2 * x + other
-        for k in range(1, XS):
-            source = (x + k) % XS
-            remote(
-                shares.at[block], across.at[other, source], xsend.at[block],
-                xrecv.at[other, source], twin,
-            ).wait_recv()
-        total = shares[block]
-        for k in range(1, XS):
-            total = total + across[other, (x + k) % XS]
         for way in range(2):
-            summed[other, way] = total[:, way * gene:(way + 1) * gene]
-
-        @pl.when(other == lo)
-        def _():
-            same.start()
-
-        @pl.when(other != lo)
-        def _():
-            both.start()
-            cross.start()
+            for k in range(1, XS):
+                source = (x + k) % XS
+                remote(
+                    shares.at[block, way], across.at[other, source, way], xsend.at[block, way],
+                    xrecv.at[other, source, way], twin,
+                ).wait_recv()
+            total = shares[block, way]
+            for k in range(1, XS):
+                total = total + across[other, (x + k) % XS, way]
+            summed[other, way] = total
+
+            @pl.when((other == lo) & (way != t))
+            def _():
+                same.start()
+
+            @pl.when((other != lo) & (way != t))
+            def _():
+                both.start()
+
+            @pl.when((other != lo) & (way == t))
+            def _():
+                cross.start()
 
     scale = 1.0 / (samples * XS * 4)
     own_rows = pl.ds(pl.multiple_of((1 - t) * gene, gene), gene)
@@ -321,13 +327,10 @@
     def drain(i, carry):
         step = 2 * i + odd
         for j in range(2 * PARTS):
-            @pl.when((step >= 1) & (step <= 7))
-            def _():
-                ring(place, 0, step, j, fore).wait_send()
-
-            @pl.when((step >= 1) & (step <= 6))
-            def _():
-                ring(place, 1, step, j, back).wait_send()
+            for flow, to in ((0, fore), (1, back)):
+                @pl.when((step >= 1) & (step < reach(flow, j)))
+                def _():
+                    ring(place, flow, step, j, to).wait_send()
 
         return carry
 
@@ -336,9 +339,11 @@
     def drain_shares(block, carry):
         @pl.when(block // 2 != x)
         def _():
-            remote(
-                shares.at[block], across.at[0, 0], xsend.at[block], xrecv.at[0, 0], twin
-            ).wait_send()
+            for way in range(2):
+                remote(
+                    shares.at[block, way], across.at[0, 0, way], xsend.at[block, way],
+                    xrecv.at[0, 0, way], twin,
+                ).wait_send()
 
         return carry
 
@@ -373,8 +378,8 @@
             pltpu.VMEM((samples, gene), F32),
             pltpu.VMEM((2 * samples, 2 * gene), BF16),
             pltpu.VMEM((ZS // 2, 2 * PARTS, gene, part), BF16),
-            pltpu.VMEM((ZS // 2, gene, 2 * gene), F32),
-            pltpu.VMEM((2, XS, gene, 2 * gene), F32),
+            pltpu.VMEM((ZS // 2, 2, gene, gene), F32),
+            pltpu.VMEM((2, XS, 2, gene, gene), F32),
             pltpu.VMEM((2, 2, gene, gene), F32),
             pltpu.VMEM((3, gene, gene), F32),
             pltpu.VMEM((PARTS, gene, part), BF16),
@@ -383,11 +388,11 @@
             dma((3, 2)), dma((3, 2)),
             dma((2, 4, 2 * PARTS)), dma((2, 5, 2 * PARTS)),
             dma((3, PARTS)), dma((PARTS,)),
-            dma((ZS // 2,)), dma((2, XS)),
+            dma((ZS // 2, 2)), dma((2, XS, 2)),
             dma((3,)), dma((3,)),
         ],
         compiler_params=pltpu.CompilerParams(
-            collective_id=0, has_side_effects=True, vmem_limit_bytes=60 * 2**20
+            collective_id=0, has_side_effects=True, vmem_limit_bytes=54800 * 1024
         ),
     )(dosage, weight_tiles, first_tile.reshape(1, gene), last_tile.reshape(1, gene))
 

time: 72.2 us -> 71.5 us (level)
    unnamed x1 -> x5, local copies, waits for them, and re-layouts: 1.57 us -> 1.33 us
where the time goes in v3:
time: 71.5 us; the launch traced here: 71.3 us
  Pallas kernels  70 us (98%)
  local copies, waits for them, and re-layouts  1.33 us (2%)
    pallas_call x1, Pallas kernels, shards(): pl.pallas_call(kernel, out_shape=jax.ShapeDtypeStruct((2 * gene, gene), F...  70 us

profile of v3, /device:TPU:44, one launch (start us, length us, event | category | flops | bytes accessed | tf_op | source)
XLA Modules:
  0.0 71.3 jit_solution(16142929342487501198)
XLA Ops:
  0.0 0.0 copy-start
  0.0 0.0 copy-start.1
  0.0 0.7 copy-done
  0.7 0.0 copy-done.1
  0.7 70.0 %shard_map.46 = f32[256,128]{1,0:T(8,128)S(1)} custom-call(bf16[512,1024]{1,0:T(8,128)(2,1)} %dosage_hbm.1, bf16[3,1024,128]{2,1,0:T(8,128)(2,1)} %tiles_hbm.1, s32[1,128]{1,0:T(1,128)S(1)} %bitcast.2, s32[1,128]{1,0:T(1,128)S(1)} %bitcast.3), custom_call_target="tpu_custom_call" | custom-call | tf_op jit(solution)/shard_map/pallas_call | solution.py:359
  70.7 0.7 copy.6
Async XLA Ops:
  0.0 0.7 copy-start
  0.0 0.7 copy-start.1
